TPU v7x, 32 devices: a whole 2x2x4 slice. The times are simulated.
32 devices in a mesh: section: 16 (over z, y, core), dp: 2 (over x).
Axes of the slice: x: 2, y: 2, z: 4, core: 2. Of those that a mesh axis runs over, the one named last changes fastest.
Arguments:
- activations: bfloat16 [16, 16, 64, 4096], P('section', 'dp'), may hold values from -6 to 6
- out_grads: bfloat16 [16, 16, 64, 4096], P('section', 'dp'), may hold values from -6 to 6
- proj_in: bfloat16 [16, 2, 4096, 128], P('section'), may hold values from -0.09375 to 0.09375
- proj_out: bfloat16 [16, 2, 64, 4096], P('section'), may hold values from -0.09375 to 0.09375
- earlier_gram: float32 [8192, 8192], P('section', 'dp'), may hold values from -4 to 4, as said below
Outputs:
- gram: float32 [8192, 8192], P('section', 'dp')
Inputs may be any that keep to these rules, and one draw needn't show every extreme that they name: earlier_gram is symmetric.
All inputs are finite; a program needn't handle non-finite values.
Results may differ from a plain program's by a relative error of at most 0.0013.
Values sent between devices are 32-bit elements; how exact they have to be, the bound alone decides.
A program may use at most 64 MiB of HBM per device.

v0:
```python
import math

import jax
import jax.numpy as jnp
from jax import lax
from jax.sharding import PartitionSpec as P

PROJ = 2
LEN = 64


def per_device(activations, out_grads, proj_in, proj_out, earlier_gram):
    layer_act = activations[0]
    layer_grad = out_grads[0]
    layer_in = proj_in[0]
    layer_out = proj_out[0]
    low_in = jnp.einsum(
        "etd,pdm->petm", layer_act, layer_in, preferred_element_type=jnp.float32
    ).astype(jnp.bfloat16)
    low_out = jnp.einsum(
        "pkd,etd->pekt", layer_out, layer_grad, preferred_element_type=jnp.float32
    ).astype(jnp.bfloat16)
    partial_terms = jnp.einsum(
        "pekt,petm->ekm", low_out, low_in, preferred_element_type=jnp.float32
    )
    local_count = partial_terms.shape[0]
    partial_terms = partial_terms.reshape(local_count, -1)
    n_layers = lax.axis_size("section")
    n_groups = lax.axis_size("dp")
    total_examples = local_count * n_groups
    scale = 1.0 / math.sqrt(LEN * n_layers * PROJ)
    row_width = earlier_gram.shape[0]
    col_width = earlier_gram.shape[1]
    row_start = lax.axis_index("section") * row_width
    col_start = lax.axis_index("dp") * col_width
    summed = lax.psum(partial_terms, "section") * scale
    features = lax.all_gather(summed, "dp", axis=0, tiled=True)
    row_block = lax.dynamic_slice_in_dim(features, row_start, row_width, 1)
    col_block = lax.dynamic_slice_in_dim(features, col_start, col_width, 1)
    outer = jnp.dot(row_block.T, col_block, precision=lax.Precision.HIGHEST)
    return earlier_gram + outer / total_examples


def solution(mesh):
    return jax.shard_map(
        per_device,
        mesh=mesh,
        in_specs=(
            P("section", "dp", None, None),
            P("section", "dp", None, None),
            P("section", None, None, None),
            P("section", None, None, None),
            P("section", "dp"),
        ),
        out_specs=P("section", "dp"),
        check_vma=False,
    )
```

profile of v0, /device:TPU:0, one launch (start us, length us, event | category | flops | bytes accessed | tf_op | source)
XLA Modules:
  0.0 136.9 jit_solution(12887768697109643629)
XLA Ops:
  6.5 0.0 copy-start
  6.5 0.0 all-reduce.2.cloned.1.call-start
  6.5 4.8 %fusion.13 = bf16[2,8,64,64]{3,2,0,1:T(8,128)(2,1)S(1)} fusion(bf16[1,8,64,4096]{3,2,1,0:T(8,128)(2,1)} %param.6, bf16[1,2,64,4096]{3,2,1,0:T(8,128)(2,1)} %param.8), kind=kOutput, calls=%fused_computation.8 | convolution fusion | flops 536936448 | bytes 5373952 | tf_op jit(solution)/shard_map/pkd,etd->pekt/dot_general | solution.py:20
  11.3 0.0 copy-done
  11.3 3.6 %convolution_bitcast_fusion = f32[1,8,64,128]{3,2,1,0:T(8,128)S(1)} fusion(bf16[2,8,64,64]{3,2,0,1:T(8,128)(2,1)S(1)} %fusion.13, bf16[1,8,64,4096]{3,2,1,0:T(8,128)(2,1)} %param.5, bf16[1,2,4096,128]{3,2,1,0:T(8,128)(2,1)S(1)} %copy-done), kind=kOutput, calls=%fused_computation.9 | convolution fusion | flops 1090650112 | bytes 6684672 | tf_op jit(solution)/shard_map/pekt,petm->ekm/dot_general | solution.py:23
  15.0 0.9 copy.11
  15.8 0.0 all-reduce.2.cloned.1.call-update
  15.9 92.6 %all-reduce.2.cloned.1.call-done = f32[8,8192]{1,0:T(8,128)} async-done(((f32[8,8192]{1,0:T(8,128)}), f32[8,8192]{1,0:T(8,128)}) %all-reduce.2.cloned.1.call-update) | async-done | bytes 262160 | tf_op jit(solution)/shard_map/psum | solution.py:36
  108.5 1.0 broadcast_multiply_fusion
  109.4 9.3 %all_gather.3 = f32[16,8192]{1,0:T(8,128)S(1)} all-gather(f32[8,8192]{1,0:T(8,128)S(1)} %broadcast_multiply_fusion), channel_id=1, replica_groups=mesh['section'=16,'dp'=2] {'dp'}, dimensions={0}, use_global_device_ids=true | all-gather | bytes 786432 | tf_op jit(solution)/shard_map/all_gather | solution.py:37
  118.8 11.3 %multiply_add_fusion = f32[512,4096]{1,0:T(8,128)} fusion(f32[512,4096]{1,0:T(8,128)} %param.9, f32[16,8192]{1,0:T(8,128)S(1)} %all_gather.3, s32[]{:T(128)S(6)} %select_n.7, s32[]{:T(128)S(6)} %select_n.6), kind=kOutput, calls=%fused_computation | convolution fusion | flops 406847488 | bytes 17072136 | tf_op jit(solution)/shard_map/dot_general | solution.py:40
Async XLA Ops:
  6.5 4.8 %copy-start = (bf16[1,2,4096,128]{3,2,1,0:T(8,128)(2,1)S(1)}, bf16[1,2,4096,128]{3,2,1,0:T(8,128)(2,1)}, u32[]{:S(2)}) copy-start(bf16[1,2,4096,128]{3,2,1,0:T(8,128)(2,1)} %param.7) | copy-start | bytes 6291460
  6.5 101.9 %all-reduce.2.cloned.1.call-start = ((), (), s32[]{:S(2)}) async-start(), calls=%async_computation | async-start | bytes 524288 | tf_op jit(solution)/shard_map/psum | solution.py:36
Sparse Core Ops, SparseCore 0:
  16.0 92.4 all-reduce.1
where the time goes:
time: 137 us
  waiting for transfers between devices  92.6 us (68%)
  matrix products  19.8 us (14%)
  between operations  13.4 us (10%)
  blocking collectives  9.31 us (7%)
    psum x1, waiting for transfers between devices, per_device(): summed = lax.psum(partial_terms, 'section') * scale  92.6 us
    dot_general x1, matrix products, per_device(): outer = jnp.dot(row_block.T, col_block, precision=lax.Precision.HIGHEST)  11.3 us
    all_gather x1, blocking collectives, per_device(): features = lax.all_gather(summed, 'dp', axis=0, tiled=True)  9.31 us
    dot_general x1, matrix products, per_device(): jnp.einsum('pkd,etd->pekt', layer_out, layer_grad, preferred_element_type...  4.78 us
    dot_general x1, matrix products, per_device(): jnp.einsum('pekt,petm->ekm', low_out, low_in, preferred_element_type=jnp....  3.63 us
  transfers between devices with their start and end apart: 1, of which 1 were waited for; matrix products, arithmetic and copies ran while one was open for 0% of the time, Pallas kernels for 0%

commit v1 on v0

v1 whole, which is shorter than its diff:
```python
import functools
import math

import jax
import jax.numpy as jnp
from jax import lax
from jax.experimental import pallas as pl
from jax.experimental.pallas import tpu as pltpu
from jax.sharding import PartitionSpec as P

MESH = pl.DeviceIdType.MESH
LANES = 128
HALVES = 2
DEPTHS = 4


def split(x):
    hi = x.astype(jnp.bfloat16)
    lo = (x - hi.astype(jnp.float32)).astype(jnp.bfloat16)
    return hi, lo


def feature_kernel(
    n, groups, count, scale,
    act, grad, p_in, p_out,
    left, right,
    act_v, grad_v, in_v, out_v, low_in, low_out,
    mine, theirs, arrived, pieces, whole, cols, row,
    load_sem, pair_sem, send_sem, recv_sem, dp_send, dp_recv,
    col_send, col_recv, fwd_send, row_sem,
):
    s = lax.axis_index("section")
    d = lax.axis_index("dp")
    chips = n // 2
    core = s % 2
    chip = s // 2
    partner = s + 1 - 2 * core

    draws, width, k_in = p_in.shape
    k_out = p_out.shape[1]
    tokens = act.shape[0]
    length = tokens // count
    rows = tokens // HALVES
    depth = width // DEPTHS

    loads = {}
    slot = 0
    for h in range(HALVES):
        for c in range(DEPTHS):
            cs = pl.ds(c * depth, depth)
            rs = pl.ds(h * rows, rows)
            wanted = []
            if h == 0:
                wanted.append(("p_in", p_in.at[:, cs], in_v.at[:, cs]))
            wanted.append(("act", act.at[rs, cs], act_v.at[rs, cs]))
            if h == 0:
                wanted.append(("p_out", p_out.at[:, :, cs], out_v.at[:, :, cs]))
            wanted.append(("grad", grad.at[rs, cs], grad_v.at[rs, cs]))
            for name, src, dst in wanted:
                copy = pltpu.make_async_copy(src, dst, load_sem.at[slot])
                copy.start()
                loads[name, h, c] = copy
                slot += 1

    barrier = pltpu.get_barrier_semaphore()
    for i in range(1, n):
        pl.semaphore_signal(barrier, inc=1, device_id={"section": (s + i) % n, "dp": d}, device_id_type=MESH)
    for j in range(1, groups):
        pl.semaphore_signal(barrier, inc=1, device_id={"section": s, "dp": (d + j) % groups}, device_id_type=MESH)

    for h in range(HALVES):
        rs = slice(h * rows, (h + 1) * rows)
        total_in = total_out = None
        for c in range(DEPTHS):
            cs = slice(c * depth, (c + 1) * depth)
            if h == 0:
                loads["p_in", h, c].wait()
            loads["act", h, c].wait()
            weights = jnp.concatenate([in_v[p, cs, :] for p in range(draws)], axis=1)
            term = jnp.dot(act_v[rs, cs], weights, preferred_element_type=jnp.float32)
            total_in = term if total_in is None else total_in + term
            if h == 0:
                loads["p_out", h, c].wait()
            loads["grad", h, c].wait()
            weights = out_v[:, :, cs].reshape(draws * k_out, depth)
            term = lax.dot_general(
                grad_v[rs, cs], weights, (((1,), (1,)), ((), ())), preferred_element_type=jnp.float32
            )
            total_out = term if total_out is None else total_out + term
        low_in[rs, :] = total_in.astype(jnp.bfloat16)
        low_out[:, rs] = total_out.T.astype(jnp.bfloat16)

    k_half = k_out // 2

    def terms(which, into):
        for e in range(count):
            ts = slice(e * length, (e + 1) * length)
            value = None
            for p in range(draws):
                start = pl.multiple_of(p * k_out + which * k_half, k_half)
                term = jnp.dot(
                    low_out[pl.ds(start, k_half), ts],
                    low_in[ts, p * k_in:(p + 1) * k_in],
                    preferred_element_type=jnp.float32,
                )
                value = term if value is None else value + term
            into[:, e, :] = value

    def remote(src, dst, ssem, rsem, section, dp):
        return pltpu.make_async_remote_copy(
            src_ref=src, dst_ref=dst, send_sem=ssem, recv_sem=rsem,
            device_id={"section": section, "dp": dp}, device_id_type=MESH,
        )

    terms(1 - core, theirs)
    pl.semaphore_wait(barrier, n - 1 + groups - 1)
    swap = remote(theirs, arrived, pair_sem.at[0], pair_sem.at[1], partner, d)
    swap.start()
    terms(core, mine)
    swap.wait_recv()

    k_chunk = k_half // chips
    sends = []
    for i in range(chips - 1, 0, -1):
        to = (chip + i) % chips
        ks = pl.ds(to * k_chunk, k_chunk)
        mine[ks] = mine[ks] + arrived[ks]
        copy = remote(mine.at[ks], pieces.at[i - 1], send_sem.at[i - 1], recv_sem.at[i - 1], 2 * to + core, d)
        copy.start()
        sends.append(copy)
    ks = pl.ds(chip * k_chunk, k_chunk)
    total = mine[ks] + arrived[ks]
    for i in range(1, chips):
        sends[chips - 1 - i].wait_recv()
        total = total + pieces[i - 1]

    def block(g):
        return pl.ds(pl.multiple_of(g * count, count), count)

    whole[:, block(d), :] = total
    for j in range(1, groups):
        to = (d + j) % groups
        copy = remote(whole.at[:, block(d), :], whole.at[:, block(d), :], dp_send.at[j - 1], dp_recv.at[j - 1], s, to)
        copy.start()
        sends.append(copy)
    for j in range(1, groups):
        origin = (d + groups - j) % groups
        remote(
            whole.at[:, block(origin), :], whole.at[:, block(origin), :], dp_send.at[j - 1], dp_recv.at[j - 1], s, origin
        ).wait_recv()

    per_group = n // groups
    q = core * chips + chip
    own_slot = q % per_group
    is_col = q // per_group == d

    def col_copies():
        copies = [remote(whole, cols.at[own_slot], col_send.at[0], col_recv.at[own_slot], partner, d)]
        for i in range(1, chips):
            to = 2 * ((chip + i) % chips) + core
            copies.append(remote(whole, cols.at[own_slot], col_send.at[i], col_recv.at[own_slot], to, d))
        return copies

    def row_copy():
        return remote(whole, row, row_sem.at[0], row_sem.at[1], q, d)

    @pl.when(is_col)
    def _():
        for copy in col_copies():
            copy.start()
        cols[own_slot] = whole[...]

    @pl.when(jnp.logical_and(jnp.logical_not(is_col), q != s))
    def _():
        row_copy().start()

    @pl.when(jnp.logical_and(jnp.logical_not(is_col), q == s))
    def _():
        row[...] = whole[...]

    def forward(j):
        return remote(cols.at[j], cols.at[j], fwd_send.at[j], col_recv.at[j], partner, d)

    for i in range(per_group):
        j = (chip + per_group * chips - i) % per_group
        owner = d * per_group + j
        owner_core = owner // chips

        @pl.when(owner != q)
        def _():
            forward(j).wait_recv()

        @pl.when(jnp.logical_and(owner != q, owner_core == core))
        def _():
            forward(j).start()

        for k in range(k_chunk):
            hi, lo = split(cols[j, k])
            at = pl.multiple_of((j * k_chunk + k) * LANES, LANES)
            right[:, pl.ds(at, LANES)] = jnp.concatenate([hi, hi, lo], axis=0)

    @pl.when(jnp.logical_and(s // per_group != d, q != s))
    def _():
        row_copy().wait_recv()

    @pl.when(s // per_group == d)
    def _():
        row[...] = cols[s % per_group]

    for k in range(k_chunk):
        hi, lo = split(row[k] * scale)
        left[:, k * LANES:(k + 1) * LANES] = jnp.concatenate([hi, lo, hi], axis=0)

    swap.wait_send()
    for copy in sends:
        copy.wait_send()

    @pl.when(is_col)
    def _():
        for copy in col_copies():
            copy.wait_send()

    @pl.when(jnp.logical_and(jnp.logical_not(is_col), q != s))
    def _():
        row_copy().wait_send()

    for j in range(per_group):
        owner = d * per_group + j

        @pl.when(jnp.logical_and(owner != q, owner // chips == core))
        def _():
            forward(j).wait_send()


def gram_kernel(tiles, left, right, earlier, out, tile_v, sem):
    columns = right.shape[1] // tiles
    lhs = left[...].T
    copies = []
    for i in range(tiles):
        cs = slice(i * columns, (i + 1) * columns)
        tile_v[:, cs] = earlier[:, cs] + jnp.dot(lhs, right[:, cs], preferred_element_type=jnp.float32)
        copy = pltpu.make_async_copy(
            tile_v.at[:, pl.ds(i * columns, columns)], out.at[:, pl.ds(i * columns, columns)], sem.at[i]
        )
        copy.start()
        copies.append(copy)
    for copy in copies:
        copy.wait()


def per_device(activations, out_grads, proj_in, proj_out, earlier_gram):
    n = lax.axis_size("section")
    groups = lax.axis_size("dp")
    _, count, length, width = activations.shape
    _, draws, _, k_in = proj_in.shape
    k_out = proj_out.shape[2]
    tokens = count * length
    examples = count * groups
    scale = 1.0 / (length * n * draws) / examples
    row_width, col_width = earlier_gram.shape
    chips = n // 2
    k_half = k_out // 2
    k_chunk = k_half // chips
    per_group = n // groups
    any_spec = pl.BlockSpec(memory_space=pl.ANY)
    vmem_spec = pl.BlockSpec(memory_space=pltpu.VMEM)
    f32, bf16 = jnp.float32, jnp.bfloat16
    dma = pltpu.SemaphoreType.DMA

    left, right = pl.pallas_call(
        functools.partial(feature_kernel, n, groups, count, scale),
        out_shape=(
            jax.ShapeDtypeStruct((3 * examples, row_width), bf16),
            jax.ShapeDtypeStruct((3 * examples, col_width), bf16),
        ),
        in_specs=[pl.BlockSpec(memory_space=pltpu.HBM)] * 4,
        out_specs=(vmem_spec, vmem_spec),
        scratch_shapes=[
            pltpu.VMEM((tokens, width), bf16),
            pltpu.VMEM((tokens, width), bf16),
            pltpu.VMEM((draws, width, k_in), bf16),
            pltpu.VMEM((draws, k_out, width), bf16),
            pltpu.VMEM((tokens, draws * k_in), bf16),
            pltpu.VMEM((draws * k_out, tokens), bf16),
            pltpu.VMEM((k_half, count, k_in), f32),
            pltpu.VMEM((k_half, count, k_in), f32),
            pltpu.VMEM((k_half, count, k_in), f32),
            pltpu.VMEM((chips - 1, k_chunk, count, k_in), f32),
            pltpu.VMEM((k_chunk, examples, k_in), f32),
            pltpu.VMEM((per_group, k_chunk, examples, k_in), f32),
            pltpu.VMEM((k_chunk, examples, k_in), f32),
            dma((2 * DEPTHS * (HALVES + 1),)),
            dma((2,)),
            dma((chips - 1,)),
            dma((chips - 1,)),
            dma((groups - 1,)),
            dma((groups - 1,)),
            dma((chips,)),
            dma((per_group,)),
            dma((per_group,)),
            dma((2,)),
        ],
        compiler_params=pltpu.CompilerParams(
            collective_id=0, has_side_effects=True, vmem_limit_bytes=28 << 20
        ),
        name="features",
    )(
        activations.reshape(tokens, width),
        out_grads.reshape(tokens, width),
        proj_in[0],
        proj_out[0],
    )
    tiles = 8
    return pl.pallas_call(
        functools.partial(gram_kernel, tiles),
        out_shape=jax.ShapeDtypeStruct((row_width, col_width), f32),
        in_specs=[vmem_spec, vmem_spec, vmem_spec],
        out_specs=any_spec,
        scratch_shapes=[pltpu.VMEM((row_width, col_width), f32), dma((tiles,))],
        compiler_params=pltpu.CompilerParams(vmem_limit_bytes=28 << 20),
        name="gram",
    )(left, right, earlier_gram)


def solution(mesh):
    return jax.shard_map(
        per_device,
        mesh=mesh,
        in_specs=(
            P("section", "dp", None, None),
            P("section", "dp", None, None),
            P("section", None, None, None),
            P("section", None, None, None),
            P("section", "dp"),
        ),
        out_specs=P("section", "dp"),
        check_vma=False,
    )
```

time: 137 us -> 36.8 us (0.27)
  waiting for transfers between devices: 92.6 us -> 0 us
  Pallas kernels: 0 us -> 29.4 us
  matrix products: 19.8 us -> 0 us
  between operations: 13.4 us -> 0.02 us
  blocking collectives: 9.31 us -> 0 us
  local copies, waits for them, and re-layouts: 0.87 us -> 7.19 us
    psum x1 -> x0, waiting for transfers between devices: 92.6 us -> none  [per_device(): summed = lax.psum(partial_terms, 'section') * scale]
    pallas_call x0 -> x2, Pallas kernels: none -> 29.4 us  [the longest x1 25.7 us: per_device(): pl.pallas_call(functools.partial(feature_kernel, n, groups, count, scale)...]
    dot_general x3 -> x0, matrix products: 19.8 us -> none  [the longest x1 11.3 us: per_device(): outer = jnp.dot(row_block.T, col_block, precision=lax.Precision.HIGHEST)]
    all_gather x1 -> x0, blocking collectives: 9.31 us -> none  [per_device(): features = lax.all_gather(summed, 'dp', axis=0, tiled=True)]
    unnamed x3 -> x10, local copies, waits for them, and re-layouts: 0.87 us -> 7.19 us
  transfers between devices with their start and end apart: 1 -> 0, of which waited for: 1 -> 0; matrix products, arithmetic and copies ran while one was open for 0% -> 0% of each run, Pallas kernels for 0% -> 0%
where the time goes in v1:
time: 36.8 us; the launch traced here: 36.6 us
  Pallas kernels  29.4 us (80%)
  local copies, waits for them, and re-layouts  7.19 us (20%)
    pallas_call x1, Pallas kernels, per_device(): pl.pallas_call(functools.partial(feature_kernel, n, groups, count, scale)...  25.7 us
    unnamed x10, local copies, waits for them, and re-layouts  7.19 us
    pallas_call x1, Pallas kernels, per_device(): pl.pallas_call(functools.partial(gram_kernel, tiles), out_shape=jax.Shape...  3.68 us

profile of v1, /device:TPU:0, one launch (start us, length us, event | category | flops | bytes accessed | tf_op | source)
XLA Modules:
  0.0 36.6 jit_solution(904140755935802823)
XLA Ops:
  0.0 0.0 copy-start.1
  0.0 2.2 %copy-done.1 = bf16[1,8,64,4096]{3,2,1,0:T(8,128)(2,1)S(1)} copy-done((bf16[1,8,64,4096]{3,2,1,0:T(8,128)(2,1)S(1)}, bf16[1,8,64,4096]{3,2,1,0:T(8,128)(2,1)}, u32[]{:S(2)}) %copy-start.1) | copy-done | bytes 4194328
  2.2 0.0 copy-start.2
  2.2 2.2 %copy-done.2 = bf16[1,8,64,4096]{3,2,1,0:T(8,128)(2,1)S(1)} copy-done((bf16[1,8,64,4096]{3,2,1,0:T(8,128)(2,1)S(1)}, bf16[1,8,64,4096]{3,2,1,0:T(8,128)(2,1)}, u32[]{:S(2)}) %copy-start.2) | copy-done | bytes 4194328
  4.4 0.0 copy-start.3
  4.4 1.6 %copy-done.3 = bf16[1,2,4096,128]{3,2,1,0:T(8,128)(2,1)S(1)} copy-done((bf16[1,2,4096,128]{3,2,1,0:T(8,128)(2,1)S(1)}, bf16[1,2,4096,128]{3,2,1,0:T(8,128)(2,1)}, u32[]{:S(2)}) %copy-start.3) | copy-done | bytes 2097176
  6.0 0.0 copy-start.4
  6.0 1.2 %copy-done.4 = bf16[1,2,64,4096]{3,2,1,0:T(8,128)(2,1)S(1)} copy-done((bf16[1,2,64,4096]{3,2,1,0:T(8,128)(2,1)S(1)}, bf16[1,2,64,4096]{3,2,1,0:T(8,128)(2,1)}, u32[]{:S(2)}) %copy-start.4) | copy-done | bytes 1048600
  7.2 0.0 copy-start
  7.2 25.7 %features.1 = (bf16[48,512]{1,0:T(8,128)(2,1)S(1)}, bf16[48,4096]{1,0:T(8,128)(2,1)S(1)}) custom-call(bf16[512,4096]{1,0:T(8,128)(2,1)S(1)} %bitcast.4, bf16[512,4096]{1,0:T(8,128)(2,1)S(1)} %bitcast.5, bf16[2,4096,128]{2,1,0:T(8,128)(2,1)S(1)} %bitcast.6, bf16[2,64,4096]{2,1,0:T(8,128)(2,1)S(1)} %bitcast.7), custom_call_target="tpu_custom_call" | custom-call | tf_op jit(solution)/shard_map/features/pallas_call | solution.py:270
  32.9 0.0 copy-done
  32.9 3.7 %gram.1 = f32[512,4096]{1,0:T(8,128)} custom-call(bf16[48,512]{1,0:T(8,128)(2,1)S(1)} %get-tuple-element.7.left, bf16[48,4096]{1,0:T(8,128)(2,1)S(1)} %get-tuple-element.8.right, f32[512,4096]{1,0:T(8,128)S(1)} %copy-done), custom_call_target="tpu_custom_call" | custom-call | tf_op jit(solution)/shard_map/gram/pallas_call | solution.py:314
Async XLA Ops:
  0.0 2.2 %copy-start.1 = (bf16[1,8,64,4096]{3,2,1,0:T(8,128)(2,1)S(1)}, bf16[1,8,64,4096]{3,2,1,0:T(8,128)(2,1)}, u32[]{:S(2)}) copy-start(bf16[1,8,64,4096]{3,2,1,0:T(8,128)(2,1)} %param.5) | copy-start | bytes 12582916
  2.2 2.2 %copy-start.2 = (bf16[1,8,64,4096]{3,2,1,0:T(8,128)(2,1)S(1)}, bf16[1,8,64,4096]{3,2,1,0:T(8,128)(2,1)}, u32[]{:S(2)}) copy-start(bf16[1,8,64,4096]{3,2,1,0:T(8,128)(2,1)} %param.6) | copy-start | bytes 12582916
  4.4 1.6 %copy-start.3 = (bf16[1,2,4096,128]{3,2,1,0:T(8,128)(2,1)S(1)}, bf16[1,2,4096,128]{3,2,1,0:T(8,128)(2,1)}, u32[]{:S(2)}) copy-start(bf16[1,2,4096,128]{3,2,1,0:T(8,128)(2,1)} %param.7) | copy-start | bytes 6291460
  6.0 1.2 %copy-start.4 = (bf16[1,2,64,4096]{3,2,1,0:T(8,128)(2,1)S(1)}, bf16[1,2,64,4096]{3,2,1,0:T(8,128)(2,1)}, u32[]{:S(2)}) copy-start(bf16[1,2,64,4096]{3,2,1,0:T(8,128)(2,1)} %param.8) | copy-start | bytes 3145732
  7.2 25.7 %copy-start = (f32[512,4096]{1,0:T(8,128)S(1)}, f32[512,4096]{1,0:T(8,128)}, u32[]{:S(2)}) copy-start(f32[512,4096]{1,0:T(8,128)} %earlier.1) | copy-start | bytes 25165828

commit v2 on v1

--- a/solution.py
+++ b/solution.py
@@ -273,7 +273,7 @@
             jax.ShapeDtypeStruct((3 * examples, row_width), bf16),
             jax.ShapeDtypeStruct((3 * examples, col_width), bf16),
         ),
-        in_specs=[pl.BlockSpec(memory_space=pltpu.HBM)] * 4,
+        in_specs=[any_spec] * 4,
         out_specs=(vmem_spec, vmem_spec),
         scratch_shapes=[
             pltpu.VMEM((tokens, width), bf16),
@@ -301,7 +301,7 @@
             dma((2,)),
         ],
         compiler_params=pltpu.CompilerParams(
-            collective_id=0, has_side_effects=True, vmem_limit_bytes=28 << 20
+            collective_id=0, has_side_effects=True, vmem_limit_bytes=53 << 20
         ),
         name="features",
     )(

time: 36.8 us -> 30 us (0.82)
  local copies, waits for them, and re-layouts: 7.19 us -> 0.01 us
  Pallas kernels: 29.4 us -> 29.8 us
    unnamed x10 -> x2, local copies, waits for them, and re-layouts: 7.19 us -> 0.01 us
    pallas_call x1, Pallas kernels: 25.7 us -> 26.2 us  [per_device(): pl.pallas_call(functools.partial(feature_kernel, n, groups, count, scale)...]
where the time goes in v2:
time: 30 us; the launch traced here: 29.9 us
  Pallas kernels  29.8 us (99%)
    pallas_call x1, Pallas kernels, per_device(): pl.pallas_call(functools.partial(feature_kernel, n, groups, count, scale)...  26.2 us
    pallas_call x1, Pallas kernels, per_device(): pl.pallas_call(functools.partial(gram_kernel, tiles), out_shape=jax.Shape...  3.68 us

profile of v2, /device:TPU:0, one launch (start us, length us, event | category | flops | bytes accessed | tf_op | source)
XLA Modules:
  0.0 29.9 jit_solution(2993753474706081660)
XLA Ops:
  0.0 0.0 copy-start
  0.0 26.2 %features.1 = (bf16[48,512]{1,0:T(8,128)(2,1)S(1)}, bf16[48,4096]{1,0:T(8,128)(2,1)S(1)}) custom-call(bf16[512,4096]{1,0:T(8,128)(2,1)} %bitcast.4, bf16[512,4096]{1,0:T(8,128)(2,1)} %bitcast.5, bf16[2,4096,128]{2,1,0:T(8,128)(2,1)} %bitcast.6, bf16[2,64,4096]{2,1,0:T(8,128)(2,1)} %bitcast.7), custom_call_target="tpu_custom_call" | custom-call | tf_op jit(solution)/shard_map/features/pallas_call | solution.py:270
  26.2 0.0 copy-done
  26.2 3.7 %gram.1 = f32[512,4096]{1,0:T(8,128)} custom-call(bf16[48,512]{1,0:T(8,128)(2,1)S(1)} %get-tuple-element.7.left, bf16[48,4096]{1,0:T(8,128)(2,1)S(1)} %get-tuple-element.8.right, f32[512,4096]{1,0:T(8,128)S(1)} %copy-done), custom_call_target="tpu_custom_call" | custom-call | tf_op jit(solution)/shard_map/gram/pallas_call | solution.py:314
Async XLA Ops:
  0.0 26.2 %copy-start = (f32[512,4096]{1,0:T(8,128)S(1)}, f32[512,4096]{1,0:T(8,128)}, u32[]{:S(2)}) copy-start(f32[512,4096]{1,0:T(8,128)} %earlier.1) | copy-start | bytes 25165828

commit v3 on v2

--- a/solution.py
+++ b/solution.py
@@ -22,12 +22,12 @@
 
 def feature_kernel(
     n, groups, count, scale,
-    act, grad, p_in, p_out,
-    left, right,
+    act, grad, p_in, p_out, earlier,
+    left, right, held,
     act_v, grad_v, in_v, out_v, low_in, low_out,
-    mine, theirs, arrived, pieces, whole, cols, row,
-    load_sem, pair_sem, send_sem, recv_sem, dp_send, dp_recv,
-    col_send, col_recv, fwd_send, row_sem,
+    mine, theirs, arrived, pieces, own, cols, row,
+    load_sem, pair_sem, send_sem, recv_sem,
+    col_send, col_recv, fwd_send, row_send, row_recv, held_sem,
 ):
     s = lax.axis_index("section")
     d = lax.axis_index("dp")
@@ -63,10 +63,11 @@
                 slot += 1
 
     barrier = pltpu.get_barrier_semaphore()
-    for i in range(1, n):
-        pl.semaphore_signal(barrier, inc=1, device_id={"section": (s + i) % n, "dp": d}, device_id_type=MESH)
-    for j in range(1, groups):
-        pl.semaphore_signal(barrier, inc=1, device_id={"section": s, "dp": (d + j) % groups}, device_id_type=MESH)
+    for g in range(groups):
+        for i in range(n):
+            if g or i:
+                peer = {"section": (s + i) % n, "dp": (d + g) % groups}
+                pl.semaphore_signal(barrier, inc=1, device_id=peer, device_id_type=MESH)
 
     for h in range(HALVES):
         rs = slice(h * rows, (h + 1) * rows)
@@ -87,6 +88,9 @@
                 grad_v[rs, cs], weights, (((1,), (1,)), ((), ())), preferred_element_type=jnp.float32
             )
             total_out = term if total_out is None else total_out + term
+        if h == HALVES - 1:
+            hold = pltpu.make_async_copy(earlier, held, held_sem)
+            hold.start()
         low_in[rs, :] = total_in.astype(jnp.bfloat16)
         low_out[:, rs] = total_out.T.astype(jnp.bfloat16)
 
@@ -113,16 +117,24 @@
         )
 
     terms(1 - core, theirs)
-    pl.semaphore_wait(barrier, n - 1 + groups - 1)
+    pl.semaphore_wait(barrier, n * groups - 1)
     swap = remote(theirs, arrived, pair_sem.at[0], pair_sem.at[1], partner, d)
     swap.start()
     terms(core, mine)
     swap.wait_recv()
 
+    def across(c, i):
+        bit = 1
+        while bit < chips:
+            if i & bit:
+                c = c + bit * (1 - 2 * ((c // bit) % 2))
+            bit *= 2
+        return c
+
     k_chunk = k_half // chips
     sends = []
     for i in range(chips - 1, 0, -1):
-        to = (chip + i) % chips
+        to = across(chip, i)
         ks = pl.ds(to * k_chunk, k_chunk)
         mine[ks] = mine[ks] + arrived[ks]
         copy = remote(mine.at[ks], pieces.at[i - 1], send_sem.at[i - 1], recv_sem.at[i - 1], 2 * to + core, d)
@@ -134,102 +146,114 @@
         sends[chips - 1 - i].wait_recv()
         total = total + pieces[i - 1]
 
-    def block(g):
-        return pl.ds(pl.multiple_of(g * count, count), count)
-
-    whole[:, block(d), :] = total
-    for j in range(1, groups):
-        to = (d + j) % groups
-        copy = remote(whole.at[:, block(d), :], whole.at[:, block(d), :], dp_send.at[j - 1], dp_recv.at[j - 1], s, to)
-        copy.start()
-        sends.append(copy)
-    for j in range(1, groups):
-        origin = (d + groups - j) % groups
-        remote(
-            whole.at[:, block(origin), :], whole.at[:, block(origin), :], dp_send.at[j - 1], dp_recv.at[j - 1], s, origin
-        ).wait_recv()
+    own[...] = total
 
     per_group = n // groups
     q = core * chips + chip
     own_slot = q % per_group
-    is_col = q // per_group == d
-
-    def col_copies():
-        copies = [remote(whole, cols.at[own_slot], col_send.at[0], col_recv.at[own_slot], partner, d)]
-        for i in range(1, chips):
-            to = 2 * ((chip + i) % chips) + core
-            copies.append(remote(whole, cols.at[own_slot], col_send.at[i], col_recv.at[own_slot], to, d))
-        return copies
-
-    def row_copy():
-        return remote(whole, row, row_sem.at[0], row_sem.at[1], q, d)
-
-    @pl.when(is_col)
-    def _():
-        for copy in col_copies():
-            copy.start()
-        cols[own_slot] = whole[...]
-
-    @pl.when(jnp.logical_and(jnp.logical_not(is_col), q != s))
-    def _():
-        row_copy().start()
-
-    @pl.when(jnp.logical_and(jnp.logical_not(is_col), q == s))
-    def _():
-        row[...] = whole[...]
-
-    def forward(j):
-        return remote(cols.at[j], cols.at[j], fwd_send.at[j], col_recv.at[j], partner, d)
+    home = q // per_group
+    at_home = home == d
+
+    def col_copy(i):
+        return remote(
+            own, cols.at[own_slot, d], col_send.at[i], col_recv.at[own_slot, d], 2 * across(chip, i) + core, home
+        )
+
+    def pair_copy():
+        return remote(own, cols.at[own_slot, d], col_send.at[0], col_recv.at[own_slot, d], partner, d)
+
+    def row_copy(g):
+        return remote(own, row.at[d], row_send.at[g], row_recv.at[d], q, g)
+
+    for i in range(chips - 1, 0, -1):
+        col_copy(i).start()
+
+    @pl.when(at_home)
+    def _():
+        pair_copy().start()
+        cols[own_slot, d] = own[...]
+
+    @pl.when(jnp.logical_not(at_home))
+    def _():
+        col_copy(0).start()
+
+    for g in range(groups):
+        needed = home != g
+        here = jnp.logical_and(q == s, d == g)
+
+        @pl.when(jnp.logical_and(needed, jnp.logical_not(here)))
+        def _():
+            row_copy(g).start()
+
+        @pl.when(jnp.logical_and(needed, here))
+        def _():
+            row[d] = own[...]
+
+    def forward(j, g):
+        return remote(cols.at[j, g], cols.at[j, g], fwd_send.at[j, g], col_recv.at[j, g], partner, d)
 
     for i in range(per_group):
-        j = (chip + per_group * chips - i) % per_group
+        j = (chip + i) % per_group
         owner = d * per_group + j
-        owner_core = owner // chips
-
-        @pl.when(owner != q)
-        def _():
-            forward(j).wait_recv()
-
-        @pl.when(jnp.logical_and(owner != q, owner_core == core))
-        def _():
-            forward(j).start()
+        for g in range(groups):
+            other = jnp.logical_or(owner != q, d != g)
+
+            @pl.when(other)
+            def _():
+                forward(j, g).wait_recv()
+
+            @pl.when(jnp.logical_and(other, owner // chips == core))
+            def _():
+                forward(j, g).start()
 
         for k in range(k_chunk):
-            hi, lo = split(cols[j, k])
+            hi, lo = split(jnp.concatenate([cols[j, g, k] for g in range(groups)], axis=0))
             at = pl.multiple_of((j * k_chunk + k) * LANES, LANES)
             right[:, pl.ds(at, LANES)] = jnp.concatenate([hi, hi, lo], axis=0)
 
-    @pl.when(jnp.logical_and(s // per_group != d, q != s))
-    def _():
-        row_copy().wait_recv()
+    for g in range(groups):
+
+        @pl.when(jnp.logical_and(s // per_group != d, jnp.logical_or(q != s, d != g)))
+        def _():
+            remote(own, row.at[g], row_send.at[g], row_recv.at[g], q, d).wait_recv()
 
     @pl.when(s // per_group == d)
     def _():
         row[...] = cols[s % per_group]
 
     for k in range(k_chunk):
-        hi, lo = split(row[k] * scale)
+        hi, lo = split(jnp.concatenate([row[g, k] for g in range(groups)], axis=0) * scale)
         left[:, k * LANES:(k + 1) * LANES] = jnp.concatenate([hi, lo, hi], axis=0)
 
+    hold.wait()
     swap.wait_send()
     for copy in sends:
         copy.wait_send()
 
-    @pl.when(is_col)
-    def _():
-        for copy in col_copies():
-            copy.wait_send()
-
-    @pl.when(jnp.logical_and(jnp.logical_not(is_col), q != s))
-    def _():
-        row_copy().wait_send()
+    for i in range(1, chips):
+        col_copy(i).wait_send()
+
+    @pl.when(at_home)
+    def _():
+        pair_copy().wait_send()
+
+    @pl.when(jnp.logical_not(at_home))
+    def _():
+        col_copy(0).wait_send()
+
+    for g in range(groups):
+
+        @pl.when(jnp.logical_and(home != g, jnp.logical_or(q != s, d != g)))
+        def _():
+            row_copy(g).wait_send()
 
     for j in range(per_group):
         owner = d * per_group + j
-
-        @pl.when(jnp.logical_and(owner != q, owner // chips == core))
-        def _():
-            forward(j).wait_send()
+        for g in range(groups):
+
+            @pl.when(jnp.logical_and(jnp.logical_or(owner != q, d != g), owner // chips == core))
+            def _():
+                forward(j, g).wait_send()
 
 
 def gram_kernel(tiles, left, right, earlier, out, tile_v, sem):
@@ -267,14 +291,15 @@
     f32, bf16 = jnp.float32, jnp.bfloat16
     dma = pltpu.SemaphoreType.DMA
 
-    left, right = pl.pallas_call(
+    left, right, held = pl.pallas_call(
         functools.partial(feature_kernel, n, groups, count, scale),
         out_shape=(
-            jax.ShapeDtypeStruct((3 * examples, row_width), bf16),
-            jax.ShapeDtypeStruct((3 * examples, col_width), bf16),
+            pltpu.VMEM((3 * examples, row_width), bf16),
+            pltpu.VMEM((3 * examples, col_width), bf16),
+            pltpu.VMEM((row_width, col_width), f32),
         ),
-        in_specs=[any_spec] * 4,
-        out_specs=(vmem_spec, vmem_spec),
+        in_specs=[any_spec] * 5,
+        out_specs=(vmem_spec, vmem_spec, vmem_spec),
         scratch_shapes=[
             pltpu.VMEM((tokens, width), bf16),
             pltpu.VMEM((tokens, width), bf16),
@@ -286,22 +311,22 @@
             pltpu.VMEM((k_half, count, k_in), f32),
             pltpu.VMEM((k_half, count, k_in), f32),
             pltpu.VMEM((chips - 1, k_chunk, count, k_in), f32),
-            pltpu.VMEM((k_chunk, examples, k_in), f32),
-            pltpu.VMEM((per_group, k_chunk, examples, k_in), f32),
-            pltpu.VMEM((k_chunk, examples, k_in), f32),
+            pltpu.VMEM((k_chunk, count, k_in), f32),
+            pltpu.VMEM((per_group, groups, k_chunk, count, k_in), f32),
+            pltpu.VMEM((groups, k_chunk, count, k_in), f32),
             dma((2 * DEPTHS * (HALVES + 1),)),
             dma((2,)),
             dma((chips - 1,)),
             dma((chips - 1,)),
-            dma((groups - 1,)),
-            dma((groups - 1,)),
             dma((chips,)),
-            dma((per_group,)),
-            dma((per_group,)),
-            dma((2,)),
+            dma((per_group, groups)),
+            dma((per_group, groups)),
+            dma((groups,)),
+            dma((groups,)),
+            dma,
         ],
         compiler_params=pltpu.CompilerParams(
-            collective_id=0, has_side_effects=True, vmem_limit_bytes=53 << 20
+            collective_id=0, has_side_effects=True, vmem_limit_bytes=52 << 20
         ),
         name="features",
     )(
@@ -309,6 +334,7 @@
         out_grads.reshape(tokens, width),
         proj_in[0],
         proj_out[0],
+        earlier_gram,
     )
     tiles = 8
     return pl.pallas_call(
@@ -319,7 +345,7 @@
         scratch_shapes=[pltpu.VMEM((row_width, col_width), f32), dma((tiles,))],
         compiler_params=pltpu.CompilerParams(vmem_limit_bytes=28 << 20),
         name="gram",
-    )(left, right, earlier_gram)
+    )(left, right, held)
 
 
 def solution(mesh):

time: 30 us -> 28.7 us (0.957)
  Pallas kernels: 29.8 us -> 28.5 us
    pallas_call x1, Pallas kernels: 26.2 us -> 24.8 us  [per_device(): pl.pallas_call(functools.partial(feature_kernel, n, groups, count, scale)...]
where the time goes in v3:
time: 28.7 us; the launch traced here: 28.5 us
  Pallas kernels  28.5 us (99%)
    pallas_call x1, Pallas kernels, per_device(): pl.pallas_call(functools.partial(feature_kernel, n, groups, count, scale)...  24.8 us
    pallas_call x1, Pallas kernels, per_device(): pl.pallas_call(functools.partial(gram_kernel, tiles), out_shape=jax.Shape...  3.68 us

profile of v3, /device:TPU:0, one launch (start us, length us, event | category | flops | bytes accessed | tf_op | source)
XLA Modules:
  0.0 28.5 jit_solution(133295587273099314)
XLA Ops:
  0.0 24.8 %features.1 = (bf16[48,512]{1,0:T(8,128)(2,1)S(1)}, bf16[48,4096]{1,0:T(8,128)(2,1)S(1)}, f32[512,4096]{1,0:T(8,128)S(1)}) custom-call(bf16[512,4096]{1,0:T(8,128)(2,1)} %bitcast.4, bf16[512,4096]{1,0:T(8,128)(2,1)} %bitcast.5, bf16[2,4096,128]{2,1,0:T(8,128)(2,1)} %bitcast.6, bf16[2,64,4096]{2,1,0:T(8,128)(2,1)} %bitcast.7, f32[512,4096]{1,0:T(8,128)} %earlier.1), custom_call_target="tpu_custom_call" | custom-call | tf_op jit(solution)/shard_map/features/pallas_call | solution.py:294
  24.8 3.7 %gram.1 = f32[512,4096]{1,0:T(8,128)} custom-call(bf16[48,512]{1,0:T(8,128)(2,1)S(1)} %get-tuple-element.8.left, bf16[48,4096]{1,0:T(8,128)(2,1)S(1)} %get-tuple-element.9.right, f32[512,4096]{1,0:T(8,128)S(1)} %get-tuple-element.10.earlier), custom_call_target="tpu_custom_call" | custom-call | tf_op jit(solution)/shard_map/gram/pallas_call | solution.py:340

commit v4 on v3

--- a/solution.py
+++ b/solution.py
@@ -11,7 +11,8 @@
 MESH = pl.DeviceIdType.MESH
 LANES = 128
 HALVES = 2
-DEPTHS = 4
+DEPTHS = 1
+WINDOW = 4
 
 
 def split(x):
@@ -58,9 +59,17 @@
             wanted.append(("grad", grad.at[rs, cs], grad_v.at[rs, cs]))
             for name, src, dst in wanted:
                 copy = pltpu.make_async_copy(src, dst, load_sem.at[slot])
-                copy.start()
                 loads[name, h, c] = copy
                 slot += 1
+    queue = list(loads.values())
+
+    def take(copy):
+        copy.wait()
+        if queue:
+            queue.pop(0).start()
+
+    for _ in range(WINDOW):
+        queue.pop(0).start()
 
     barrier = pltpu.get_barrier_semaphore()
     for g in range(groups):
@@ -75,14 +84,14 @@
         for c in range(DEPTHS):
             cs = slice(c * depth, (c + 1) * depth)
             if h == 0:
-                loads["p_in", h, c].wait()
-            loads["act", h, c].wait()
+                take(loads["p_in", h, c])
+            take(loads["act", h, c])
             weights = jnp.concatenate([in_v[p, cs, :] for p in range(draws)], axis=1)
             term = jnp.dot(act_v[rs, cs], weights, preferred_element_type=jnp.float32)
             total_in = term if total_in is None else total_in + term
             if h == 0:
-                loads["p_out", h, c].wait()
-            loads["grad", h, c].wait()
+                take(loads["p_out", h, c])
+            take(loads["grad", h, c])
             weights = out_v[:, :, cs].reshape(draws * k_out, depth)
             term = lax.dot_general(
                 grad_v[rs, cs], weights, (((1,), (1,)), ((), ())), preferred_element_type=jnp.float32
@@ -193,7 +202,7 @@
         return remote(cols.at[j, g], cols.at[j, g], fwd_send.at[j, g], col_recv.at[j, g], partner, d)
 
     for i in range(per_group):
-        j = (chip + i) % per_group
+        j = across(chip, i) % per_group
         owner = d * per_group + j
         for g in range(groups):
             other = jnp.logical_or(owner != q, d != g)

time: 28.7 us -> 28.5 us (level)
  no operation moved by 1% of the time
where the time goes in v4:
time: 28.5 us; the launch traced here: 28.4 us
  Pallas kernels  28.4 us (100%)
    pallas_call x1, Pallas kernels, per_device(): pl.pallas_call(functools.partial(feature_kernel, n, groups, count, scale)...  24.7 us
    pallas_call x1, Pallas kernels, per_device(): pl.pallas_call(functools.partial(gram_kernel, tiles), out_shape=jax.Shape...  3.69 us

profile of v4, /device:TPU:0, one launch (start us, length us, event | category | flops | bytes accessed | tf_op | source)
XLA Modules:
  0.0 28.4 jit_solution(11641533325137412328)
XLA Ops:
  0.0 24.7 %features.1 = (bf16[48,512]{1,0:T(8,128)(2,1)S(1)}, bf16[48,4096]{1,0:T(8,128)(2,1)S(1)}, f32[512,4096]{1,0:T(8,128)S(1)}) custom-call(bf16[512,4096]{1,0:T(8,128)(2,1)} %bitcast.4, bf16[512,4096]{1,0:T(8,128)(2,1)} %bitcast.5, bf16[2,4096,128]{2,1,0:T(8,128)(2,1)} %bitcast.6, bf16[2,64,4096]{2,1,0:T(8,128)(2,1)} %bitcast.7, f32[512,4096]{1,0:T(8,128)} %earlier.1), custom_call_target="tpu_custom_call" | custom-call | tf_op jit(solution)/shard_map/features/pallas_call | solution.py:303
  24.7 3.7 %gram.1 = f32[512,4096]{1,0:T(8,128)} custom-call(bf16[48,512]{1,0:T(8,128)(2,1)S(1)} %get-tuple-element.8.left, bf16[48,4096]{1,0:T(8,128)(2,1)S(1)} %get-tuple-element.9.right, f32[512,4096]{1,0:T(8,128)S(1)} %get-tuple-element.10.earlier), custom_call_target="tpu_custom_call" | custom-call | tf_op jit(solution)/shard_map/gram/pallas_call | solution.py:349
